TPU v7x, 32 devices: a whole 2x2x4 slice. The times are simulated.
32 devices in a mesh: ia: 2 (over x), ja: 16 (over z, y, core).
Axes of the slice: x: 2, y: 2, z: 4, core: 2. Of those that a mesh axis runs over, the one named last changes fastest.
Arguments:
- phase_space: float32 [6, 32768], P(None, 'ja'), may hold values from -8 to 8, as said below
- derivatives: float32 [6, 32768], P(None, 'ja'), may hold values from -4 to 4
- potential: float32 [32768], P('ja'), may hold values from -4.5 to -0.5
- weights: float32 [32768], P('ja'), may hold values from 0.2 to 5
- levels: int32 [32768], P('ja'), may hold values from 0 to 7
- phases: float32 [32768], P('ja'), may hold values from 0.25 to 1
- active_index: int32 [2, 4096], P('ia'), may hold values from 0 to 32767, as said below
- active_count: int32 [2], P('ia'), may hold values from 512 to 4096, as said below
Outputs:
- new_phase_space: float32 [6, 32768], P(None, 'ja')
- new_derivatives: float32 [6, 32768], P(None, 'ja')
- new_potential: float32 [32768], P('ja')
- totals: float32 [5], replicated
Inputs may be any that keep to these rules, and one draw needn't show every extreme that they name: `phase_space`: positions lie within the range and velocities likewise. `active_index`: all 8192 entries are distinct star indices; in row g only the first active_count[g] entries are active stars, the rest are to be ignored. `active_count`: one list holds exactly 4096 active stars and each other between 512 and 1536.
All inputs are finite; a program needn't handle non-finite values.
Results may differ from a plain program's by a relative error of at most 0.0003.
Values sent between devices are 32-bit elements; how exact they have to be, the bound alone decides.
No kernel may reach another device: no remote copies, remote signals or barrier semaphores. Data moves between devices by JAX's collectives and lax.ppermute only.
A program may use at most 64 MiB of HBM per device.

v0:
```python
import math
import jax
import jax.numpy as jnp
from jax import lax
from jax.sharding import PartitionSpec as P

SOFTEN = 0.01
STEP_MAX = 0.5


def elapsed(levels, phases):
    return STEP_MAX * jnp.exp2(-levels.astype(jnp.float32)) * phases


def predict(phase_rows, deriv_rows, since_last):
    position = phase_rows[0:3]
    velocity = phase_rows[3:6]
    accel = deriv_rows[0:3]
    jerk_rate = deriv_rows[3:6]
    moved = position + since_last * (
        velocity + since_last * (accel * 0.5 + since_last * jerk_rate / 6.0)
    )
    turned = velocity + since_last * (accel + since_last * jerk_rate * 0.5)
    return (moved, turned)


def pair_block(block_pos, block_vel, block_ids, source_pos, source_vel, source_mass, source_ids):
    separation = source_pos[:, None, :] - block_pos[:, :, None]
    relative = source_vel[:, None, :] - block_vel[:, :, None]
    radius_sq = jnp.sum(separation * separation, 0) + SOFTEN
    inverse = 1.0 / jnp.sqrt(radius_sq)
    weighted = jnp.where(
        source_ids[None, :] == block_ids[:, None], 0.0, source_mass[None, :] * inverse
    )
    cubed = weighted * inverse * inverse
    radial = 3.0 * jnp.sum(separation * relative, 0) / radius_sq
    accel = jnp.sum(cubed * separation, 2)
    jerk_rate = jnp.sum(cubed * (relative - radial * separation), 2)
    binding = -jnp.sum(weighted, 1)
    return (accel, jerk_rate, binding)


def field_on(
    target_pos, target_vel, target_ids, source_pos, source_vel, source_mass, source_ids, block_len
):
    row_count = target_pos.shape[1]
    block_len = math.gcd(row_count, block_len)
    block_count = row_count // block_len

    def per_block(pieces):
        return pair_block(
            pieces[0], pieces[1], pieces[2], source_pos, source_vel, source_mass, source_ids
        )

    pieces = (
        jnp.transpose(target_pos.reshape(3, block_count, block_len), (1, 0, 2)),
        jnp.transpose(target_vel.reshape(3, block_count, block_len), (1, 0, 2)),
        target_ids.reshape(block_count, block_len),
    )
    accel, jerk_rate, binding = lax.map(per_block, pieces)
    accel = jnp.transpose(accel, (1, 0, 2)).reshape(3, row_count)
    jerk_rate = jnp.transpose(jerk_rate, (1, 0, 2)).reshape(3, row_count)
    binding = binding.reshape(1, row_count)
    return jnp.concatenate([accel, jerk_rate, binding], 0)


def correct(old_rows, field_rows):
    step_size = old_rows[14]
    old_pos = old_rows[0:3]
    old_vel = old_rows[3:6]
    old_acc = old_rows[6:9]
    old_jerk = old_rows[9:12]
    new_acc = field_rows[0:3]
    new_jerk = field_rows[3:6]
    new_vel = (
        old_vel
        + step_size * 0.5 * (old_acc + new_acc)
        + step_size * step_size / 12.0 * (old_jerk - new_jerk)
    )
    new_pos = (
        old_pos
        + step_size * 0.5 * (old_vel + new_vel)
        + step_size * step_size / 12.0 * (old_acc - new_acc)
    )
    return jnp.concatenate([new_pos, new_vel, new_acc, new_jerk, field_rows[6:7]], 0)


def star_terms(position, velocity, binding, star_mass):
    kinetic = 0.5 * star_mass * jnp.sum(velocity * velocity, 0)
    depth = 0.5 * star_mass * binding
    spin = jnp.stack(
        [
            position[1] * velocity[2] - position[2] * velocity[1],
            position[2] * velocity[0] - position[0] * velocity[2],
            position[0] * velocity[1] - position[1] * velocity[0],
        ],
        0,
    )
    return jnp.concatenate([kinetic[None], depth[None], star_mass[None] * spin], 0)


def reduce_field(partial_value, active_ids, is_alive):
    field_rows = lax.psum(partial_value, "ja")
    start = jnp.int32(0)
    return (field_rows, jnp.where(is_alive, active_ids, -1), is_alive, start)


def place_rows(base_rows, gathered, gathered_ids, shard, shard_len):
    target_col = gathered_ids - shard * shard_len
    keep_rows = (gathered_ids >= 0) & (target_col >= 0) & (target_col < shard_len)
    target = jnp.where(keep_rows, target_col, shard_len)
    return base_rows.at[:, target].set(gathered, mode="drop")


def per_device(
    phase_space, derivatives, potential, weights, levels, phases, active_index, active_count
):
    shard_len = phase_space.shape[1]
    shard_size = lax.axis_size("ja")
    star_count = shard_len * shard_size
    shard = lax.axis_index("ja")
    slot_count = active_index.shape[1]
    star_mass = weights / star_count
    since_last = elapsed(levels, phases)
    moved, turned = predict(phase_space, derivatives, since_last)
    star_ids = shard * shard_len + jnp.arange(shard_len, dtype=jnp.int32)
    active_ids = active_index[0]
    is_alive = jnp.arange(slot_count, dtype=jnp.int32) < active_count[0]
    local_col = active_ids - shard * shard_len
    is_local = (local_col >= 0) & (local_col < shard_len)
    safe_col = jnp.clip(local_col, 0, shard_len - 1)
    state_rows = jnp.concatenate(
        [phase_space, derivatives, potential[None], star_mass[None], since_last[None]], 0
    )
    base_rows = jnp.concatenate([phase_space, derivatives, potential[None]], 0)
    picked = jnp.where(is_local[None, :], jnp.take(state_rows, safe_col, axis=1), 0.0)
    old_sums = jnp.sum(star_terms(phase_space[0:3], phase_space[3:6], potential, star_mass), 1)
    fetched, old_total = lax.psum((picked, old_sums), "ja")
    block_pos, block_vel = predict(fetched[0:6], fetched[6:12], fetched[14])
    partial_value = field_on(
        block_pos, block_vel, active_ids, moved, turned, star_mass, star_ids, 256
    )
    field_rows, share_ids, share_alive, start = reduce_field(partial_value, active_ids, is_alive)
    updated = correct(fetched, field_rows)
    change = star_terms(updated[0:3], updated[3:6], updated[12], fetched[13]) - star_terms(
        fetched[0:3], fetched[3:6], fetched[12], fetched[13]
    )
    payload = jnp.concatenate([updated, jnp.where(share_alive[None, :], change, 0.0)], 0)
    gathered, gathered_ids = (
        lax.all_gather(payload, "ia", axis=1, tiled=True),
        lax.all_gather(share_ids, "ia", axis=0, tiled=True),
    )
    new_state = place_rows(base_rows, gathered[0:13], gathered_ids, shard, shard_len)
    totals = old_total + jnp.sum(gathered[13:18], 1)
    return (new_state[0:6], new_state[6:12], new_state[12], totals)


def solution(mesh):
    placed = (
        P(None, "ja"),
        P(None, "ja"),
        P("ja"),
        P("ja"),
        P("ja"),
        P("ja"),
        P("ia", None),
        P("ia"),
    )
    return jax.shard_map(
        per_device,
        mesh=mesh,
        in_specs=placed,
        out_specs=(P(None, "ja"), P(None, "ja"), P("ja"), P()),
        check_vma=False,
    )
```

profile of v0, /device:TPU:0, one launch (start us, length us, event | category | flops | bytes accessed | tf_op | source)
XLA Modules:
  0.0 349.2 jit_solution(14010528817504141636)
XLA Ops:
  9.5 1.0 multiply_add_fusion.3
  11.2 2.6 concatenate.23
  14.2 10.8 %gather_fusion = f32[4096,15]{1,0:T(8,128)S(1)} fusion(f32[15,2048]{0,1:T(8,128)S(1)} %copy.113, s32[4096]{0:T(1024)S(1)} %broadcast_clamp_fusion), kind=kCustom, calls=%fused_computation | custom fusion | bytes 507904 | tf_op jit(solution)/shard_map/jit(_take)/gather | solution.py:136
  28.5 5.3 %all_gather.6 = s32[8192]{0:T(1024)S(1)} all-gather(s32[4096]{0:T(1024)S(1)} %broadcast_select_fusion), channel_id=1, replica_groups=mesh['ia'=2,'ja'=16] {'ia'}, dimensions={0}, use_global_device_ids=true | all-gather | bytes 49152 | tf_op jit(solution)/shard_map/all_gather | solution.py:151
  34.3 32.9 %psum.23 = f32[5]{0:T(128)S(1)} all-reduce(f32[5]{0:T(128)S(1)} %maximum_reduce_fusion), channel_id=1, replica_groups=mesh['ia'=2,'ja'=16] {'ja'}, use_global_device_ids=true, to_apply=%region_14.15 | all-reduce | flops 5 | bytes 40 | tf_op jit(solution)/shard_map/psum | solution.py:138
  67.3 51.7 %all-reduce.3.cloned.1.call-done = f32[15,4096]{1,0:T(8,128)} async-done(((f32[15,4096]{1,0:T(8,128)}), f32[15,4096]{1,0:T(8,128)}) %all-reduce.3.cloned.1.call-update) | async-done | bytes 245776 | tf_op jit(solution)/shard_map/psum | solution.py:138
  119.0 1.1 slice_multiply_fusion.2
  120.1 1.2 multiply_add_fusion.1
  121.3 85.2 %while.15 = (s32[]{:T(128)}, f32[16,3,256]{2,1,0:T(4,128)S(1)}, f32[16,3,256]{2,1,0:T(4,128)S(1)}, f32[16,256]{1,0:T(8,128)S(1)}, s32[16,256]{1,0:T(8,128)S(1)},...) while((s32[]{:T(128)}, f32[16,3,256]{2,1,0:T(4,128)S(1)}, ...), condition=%wide.region_7.8_spmd.clone, body=%wide.region_1.7_spmd.clone.sunk | while | flops 25690624 | bytes 16955540 | solution.py:60
  121.4 2.1 fusion.18
  123.5 0.9 fusion.19
  124.4 2.2 fusion.20
  126.7 2.1 fusion.18
  128.8 0.9 fusion.19
  129.7 2.2 fusion.20
  132.0 2.1 fusion.18
  134.2 0.9 fusion.19
  135.0 2.2 fusion.20
  137.4 2.1 fusion.18
  139.5 0.9 fusion.19
  140.4 2.2 fusion.20
  142.7 2.1 fusion.18
  144.8 0.9 fusion.19
  145.7 2.2 fusion.20
  148.0 2.1 fusion.18
  150.1 0.9 fusion.19
  151.0 2.2 fusion.20
  153.3 2.1 fusion.18
  155.5 0.9 fusion.19
  156.3 2.2 fusion.20
  158.7 2.1 fusion.18
  161.7 2.2 fusion.20
  164.0 2.1 fusion.18
  166.1 0.9 fusion.19
  167.0 2.2 fusion.20
  169.3 2.1 fusion.18
  172.3 2.2 fusion.20
  174.6 2.1 fusion.18
  176.8 0.9 fusion.19
  177.6 2.2 fusion.20
  180.0 2.1 fusion.18
  183.0 2.2 fusion.20
  185.3 2.1 fusion.18
  188.3 2.2 fusion.20
  190.6 2.1 fusion.18
  193.6 2.2 fusion.20
  196.0 2.1 fusion.18
  199.0 2.2 fusion.20
  201.3 2.1 fusion.18
  203.4 0.9 fusion.19
  204.3 2.2 fusion.20
  207.3 88.8 %all-reduce.5.cloned.1.call-done = f32[7,4096]{1,0:T(8,128)} async-done(((f32[7,4096]{1,0:T(8,128)}), f32[7,4096]{1,0:T(8,128)}) %all-reduce.5.cloned.1.call-update) | async-done | bytes 114704 | tf_op jit(solution)/shard_map/psum | solution.py:103
  296.1 1.1 multiply_reduce_fusion.1
  297.3 1.0 multiply_add_fusion
  298.3 1.0 fusion.11
  299.6 1.0 pad_maximum_fusion
  300.6 11.8 %all_gather.7 = f32[18,8192]{1,0:T(8,128)S(1)} all-gather(f32[18,4096]{1,0:T(8,128)S(1)} %pad_maximum_fusion), channel_id=1, replica_groups=mesh['ia'=2,'ja'=16] {'ia'}, dimensions={1}, use_global_device_ids=true | all-gather | bytes 884736 | tf_op jit(solution)/shard_map/all_gather | solution.py:150
  312.4 0.9 copy-done
  313.3 2.6 copy.118
  315.9 21.2 %scatter_fusion = f32[13,2048]{0,1:T(8,128)S(1)} fusion(f32[13,2048]{0,1:T(8,128)S(1)} %copy.117, s32[8192]{0:T(1024)S(1)} %compare_select_fusion.1, f32[8192,13]{1,0:T(8,128)} %copy.118), kind=kCustom, calls=%fused_computation.1 | custom fusion | bytes 1310720 | tf_op jit(solution)/shard_map/scatter | solution.py:112
  337.5 1.2 slice_reduce_fusion
  338.7 1.2 slice_reduce_fusion.1
  339.9 1.0 copy.119
  340.9 1.0 copy.120
  (164 shorter events, 15.4 us)
Async XLA Ops:
  7.2 111.8 %all-reduce.3.cloned.1.call-start = ((), (), s32[]{:S(2)}) async-start(), calls=%async_computation | async-start | bytes 524288 | tf_op jit(solution)/shard_map/psum | solution.py:138
  14.1 11.5 %copy-start.4 = (s32[1,4096]{1,0:T(1,128)S(1)}, s32[1,4096]{1,0:T(1,128)}, u32[]{:S(2)}) copy-start(s32[1,4096]{1,0:T(1,128)} %param.16) | copy-start | bytes 49156
  24.9 1.5 copy-start.2
  25.0 1.5 copy-start.3
  25.0 1.5 copy-start.5
  26.4 269.7 %all-reduce.5.cloned.1.call-start = ((), (), s32[]{:S(2)}) async-start(), calls=%async_computation.1 | async-start | bytes 262144 | tf_op jit(solution)/shard_map/psum | solution.py:103
  121.3 174.8 %copy-start.1 = (f32[15,4096]{1,0:T(8,128)S(1)}, f32[15,4096]{1,0:T(8,128)}, u32[]{:S(2)}) copy-start(f32[15,4096]{1,0:T(8,128)} %all-reduce.3.cloned.1.call-done) | copy-start | bytes 737284
  312.4 0.9 copy-start
Sparse Core Ops, SparseCore 0:
  26.5 92.4 all-reduce.2
  207.4 88.6 all-reduce.4
where the time goes:
time: 350 us; the launch traced here: 349 us
  waiting for transfers between devices  141 us (40%)
  other arithmetic  97.5 us (28%)
  blocking collectives  50 us (14%)
  local copies, waits for them, and re-layouts  44.9 us (13%)
  between operations  14.9 us (4%)
    psum x1, waiting for transfers between devices, reduce_field(): field_rows = lax.psum(partial_value, 'ja')  88.8 us
    psum x1, waiting for transfers between devices, per_device(): fetched, old_total = lax.psum((picked, old_sums), 'ja')  51.7 us
    reduce_sum x16, other arithmetic, pair_block(): jerk_rate = jnp.sum(cubed * (relative - radial * separation), 2)  35.1 us
    reduce_sum x16, other arithmetic, pair_block(): radial = 3.0 * jnp.sum(separation * relative, 0) / radius_sq  33.4 us
    psum x1, blocking collectives, per_device(): fetched, old_total = lax.psum((picked, old_sums), 'ja')  32.9 us
    scatter x1, local copies, waits for them, and re-layouts, place_rows(): return base_rows.at[:, target].set(gathered, mode='drop')  21.2 us
    reduce_sum x16, other arithmetic, pair_block(): binding = -jnp.sum(weighted, 1)  14 us
    all_gather x1, blocking collectives, per_device(): lax.all_gather(payload, 'ia', axis=1, tiled=True)  11.8 us
  transfers between devices with their start and end apart: 2, of which 2 were waited for; matrix products, arithmetic and copies ran while one was open for 1% of the time, Pallas kernels for 0%

commit v1 on v0

--- a/solution.py
+++ b/solution.py
@@ -100,7 +100,7 @@
 
 
 def reduce_field(partial_value, active_ids, is_alive):
-    field_rows = lax.psum(partial_value, "ja")
+    field_rows = jnp.sum(lax.all_gather(partial_value, "ja"), axis=0)
     start = jnp.int32(0)
     return (field_rows, jnp.where(is_alive, active_ids, -1), is_alive, start)
 

time: 350 us -> 301 us (0.86)
  waiting for transfers between devices: 141 us -> 95.5 us
    psum x1 -> x0, waiting for transfers between devices: 88.8 us -> none  [reduce_field(): field_rows = lax.psum(partial_value, 'ja')]
    psum x1, waiting for transfers between devices: 51.7 us -> 91.3 us  [per_device(): fetched, old_total = lax.psum((picked, old_sums), 'ja')]
    all_gather x0 -> x1, waiting for transfers between devices: none -> 4.22 us  [reduce_field(): field_rows = jnp.sum(lax.all_gather(partial_value, 'ja'), axis=0)]
where the time goes in v1:
time: 301 us
  other arithmetic  95.5 us (32%)
  waiting for transfers between devices  95.5 us (32%)
  blocking collectives  48.5 us (16%)
  local copies, waits for them, and re-layouts  44.9 us (15%)
  between operations  15 us (5%)
    psum x1, waiting for transfers between devices, per_device(): fetched, old_total = lax.psum((picked, old_sums), 'ja')  91.3 us
    reduce_sum x16, other arithmetic, pair_block(): jerk_rate = jnp.sum(cubed * (relative - radial * separation), 2)  35.1 us
    reduce_sum x16, other arithmetic, pair_block(): radial = 3.0 * jnp.sum(separation * relative, 0) / radius_sq  33.4 us
    psum x1, blocking collectives, per_device(): fetched, old_total = lax.psum((picked, old_sums), 'ja')  32.2 us
    scatter x1, local copies, waits for them, and re-layouts, place_rows(): return base_rows.at[:, target].set(gathered, mode='drop')  21.2 us
    reduce_sum x16, other arithmetic, pair_block(): binding = -jnp.sum(weighted, 1)  14 us
    all_gather x1, blocking collectives, per_device(): lax.all_gather(payload, 'ia', axis=1, tiled=True)  11.9 us
    gather x2, local copies, waits for them, and re-layouts, per_device(): jnp.take(state_rows, safe_col, axis=1)  11.4 us
  transfers between devices with their start and end apart: 2, of which 2 were waited for; matrix products, arithmetic and copies ran while one was open for 1% of the time, Pallas kernels for 0%

profile of v1, /device:TPU:0, one launch (start us, length us, event | category | flops | bytes accessed | tf_op | source)
XLA Modules:
  0.0 300.7 jit_solution(8879476847903044437)
XLA Ops:
  9.5 1.0 multiply_add_fusion.3
  11.2 2.6 concatenate.23
  14.2 10.8 %gather_fusion = f32[4096,15]{1,0:T(8,128)S(1)} fusion(f32[15,2048]{0,1:T(8,128)S(1)} %copy.144, s32[4096]{0:T(1024)S(1)} %broadcast_clamp_fusion), kind=kCustom, calls=%fused_computation | custom fusion | bytes 507904 | tf_op jit(solution)/shard_map/jit(_take)/gather | solution.py:136
  27.7 91.3 %all-reduce.2.cloned.1.call-done = f32[15,4096]{1,0:T(8,128)} async-done(((f32[15,4096]{1,0:T(8,128)}), f32[15,4096]{1,0:T(8,128)}) %all-reduce.2.cloned.1.call-update) | async-done | bytes 245776 | tf_op jit(solution)/shard_map/psum | solution.py:138
  118.9 1.1 slice_multiply_fusion.2
  120.0 1.2 multiply_add_fusion.1
  121.3 85.2 %while.15 = (s32[]{:T(128)}, f32[16,3,256]{2,1,0:T(4,128)S(1)}, f32[16,3,256]{2,1,0:T(4,128)S(1)}, f32[16,256]{1,0:T(8,128)S(1)}, s32[16,256]{1,0:T(8,128)S(1)},...) while((s32[]{:T(128)}, f32[16,3,256]{2,1,0:T(4,128)S(1)}, ...), condition=%wide.region_7.8_spmd.clone, body=%wide.region_1.7_spmd.clone.sunk | while | flops 25690624 | bytes 16955540 | solution.py:60
  121.3 2.1 fusion.18
  123.4 0.9 fusion.19
  124.3 2.2 fusion.20
  126.6 2.1 fusion.18
  128.8 0.9 fusion.19
  129.6 2.2 fusion.20
  132.0 2.1 fusion.18
  134.1 0.9 fusion.19
  135.0 2.2 fusion.20
  137.3 2.1 fusion.18
  139.4 0.9 fusion.19
  140.3 2.2 fusion.20
  142.6 2.1 fusion.18
  144.8 0.9 fusion.19
  145.6 2.2 fusion.20
  148.0 2.1 fusion.18
  150.1 0.9 fusion.19
  151.0 2.2 fusion.20
  153.3 2.1 fusion.18
  155.4 0.9 fusion.19
  156.3 2.2 fusion.20
  158.6 2.1 fusion.18
  160.7 0.9 fusion.19
  161.6 2.2 fusion.20
  163.9 2.1 fusion.18
  166.1 0.9 fusion.19
  166.9 2.2 fusion.20
  169.3 2.1 fusion.18
  171.4 0.9 fusion.19
  172.3 2.2 fusion.20
  174.6 2.1 fusion.18
  176.7 0.9 fusion.19
  177.6 2.2 fusion.20
  179.9 2.1 fusion.18
  182.9 2.2 fusion.20
  185.2 2.1 fusion.18
  188.2 2.2 fusion.20
  190.6 2.1 fusion.18
  192.7 0.9 fusion.19
  193.6 2.2 fusion.20
  195.9 2.1 fusion.18
  198.9 2.2 fusion.20
  201.2 2.1 fusion.18
  203.4 0.9 fusion.19
  204.2 2.2 fusion.20
  207.5 32.2 %psum.15 = f32[5]{0:T(128)S(1)} all-reduce(f32[5]{0:T(128)S(1)} %maximum_reduce_fusion), channel_id=1, replica_groups=mesh['ia'=2,'ja'=16] {'ja'}, use_global_device_ids=true, to_apply=%region_14.15 | all-reduce | flops 5 | bytes 40 | tf_op jit(solution)/shard_map/psum | solution.py:138
  240.8 4.4 %all_gather.12 = s32[8192]{0:T(1024)S(1)} all-gather(s32[4096]{0:T(1024)S(1)} %broadcast_select_fusion), channel_id=1, replica_groups=mesh['ia'=2,'ja'=16] {'ia'}, dimensions={0}, use_global_device_ids=true | all-gather | bytes 49152 | tf_op jit(solution)/shard_map/all_gather | solution.py:151
  245.2 4.2 %all-gather.4.cloned.1.call-done = f32[16,7,4096]{2,1,0:T(8,128)} async-done(((f32[1,7,4096]{2,1,0:T(8,128)}), f32[16,7,4096]{2,1,0:T(8,128)}) %all-gather.4.cloned.1.call-update) | async-done | bytes 1835024 | tf_op jit(solution)/shard_map/all_gather | solution.py:103
  249.4 1.7 reduce_sum.103
  251.9 11.9 %all_gather.15 = f32[18,8192]{1,0:T(8,128)S(1)} all-gather(f32[18,4096]{1,0:T(8,128)S(1)} %pad_maximum_fusion), channel_id=1, replica_groups=mesh['ia'=2,'ja'=16] {'ia'}, dimensions={1}, use_global_device_ids=true | all-gather | bytes 884736 | tf_op jit(solution)/shard_map/all_gather | solution.py:150
  263.9 0.9 copy-done
  264.8 2.6 copy.149
  267.4 21.2 %scatter_fusion = f32[13,2048]{0,1:T(8,128)S(1)} fusion(f32[13,2048]{0,1:T(8,128)S(1)} %copy.148, s32[8192]{0:T(1024)S(1)} %compare_select_fusion.1, f32[8192,13]{1,0:T(8,128)} %copy.149), kind=kCustom, calls=%fused_computation.1 | custom fusion | bytes 1310720 | tf_op jit(solution)/shard_map/scatter | solution.py:112
  289.0 1.2 slice_reduce_fusion
  290.2 1.2 slice_reduce_fusion.1
  291.4 1.0 copy.150
  292.4 1.0 copy.151
  (165 shorter events, 13.2 us)
Async XLA Ops:
  7.2 111.8 %all-reduce.2.cloned.1.call-start = ((), (), s32[]{:S(2)}) async-start(), calls=%async_computation | async-start | bytes 524288 | tf_op jit(solution)/shard_map/psum | solution.py:138
  14.1 11.4 %copy-start.4 = (s32[1,4096]{1,0:T(1,128)S(1)}, s32[1,4096]{1,0:T(1,128)}, u32[]{:S(2)}) copy-start(s32[1,4096]{1,0:T(1,128)} %param.16) | copy-start | bytes 49156
  26.4 223.1 %all-gather.4.cloned.1.call-start = ((), (), s32[]{:S(2)}) async-start(), calls=%async_computation.1 | async-start | bytes 2228224 | tf_op jit(solution)/shard_map/all_gather | solution.py:103
  121.2 86.0 %copy-start.2 = (f32[6,2048]{1,0:T(8,128)S(1)}, f32[6,2048]{1,0:T(8,128)}, u32[]{:S(2)}) copy-start(f32[6,2048]{1,0:T(8,128)} %param.10) | copy-start | bytes 147460
  121.2 119.1 %copy-start.3 = (f32[6,2048]{1,0:T(8,128)S(1)}, f32[6,2048]{1,0:T(8,128)}, u32[]{:S(2)}) copy-start(f32[6,2048]{1,0:T(8,128)} %param.11) | copy-start | bytes 147460
  121.3 119.1 %copy-start.5 = (f32[2048]{0:T(1024)S(1)}, f32[2048]{0:T(1024)}, u32[]{:S(2)}) copy-start(f32[2048]{0:T(1024)} %param.12) | copy-start | bytes 24580
  207.2 44.0 %copy-start.1 = (f32[15,4096]{1,0:T(8,128)S(1)}, f32[15,4096]{1,0:T(8,128)}, u32[]{:S(2)}) copy-start(f32[15,4096]{1,0:T(8,128)} %all-reduce.2.cloned.1.call-done) | copy-start | bytes 737284
  263.9 0.9 copy-start
Sparse Core Ops, SparseCore 0:
  26.5 92.4 all-reduce.1
  207.4 42.0 all-gather.3
